TPU v7x, 32 devices: a whole 2x2x4 slice. The times are simulated.
32 devices in a mesh: blk: 16 (over z, y, core), dp: 2 (over x).
Axes of the slice: x: 2, y: 2, z: 4, core: 2. Of those that a mesh axis runs over, the one named last changes fastest.
Arguments:
- tokens: bfloat16 [4096, 3584], P(('blk', 'dp')), may hold values from -6 to 6
- route_dir: int32 [4096, 1], P(('blk', 'dp')), may hold values from 0 to 2; in each aligned block of 128 rows (0 to 127, 128 to 255, ...) at most 64 rows name the same one
- gate_probs: float32 [4096, 1], P(('blk', 'dp')), may hold values from 0.3 to 1
- gate_weight: bfloat16 [16, 3584, 512], P('blk', 'dp'), may hold values from -0.09375 to 0.09375
- up_weight: bfloat16 [16, 3584, 512], P('blk', 'dp'), may hold values from -0.09375 to 0.09375
- down_weight: bfloat16 [16, 3584, 512], P('blk', 'dp'), may hold values from -0.1875 to 0.1875
Outputs:
- d_tokens: bfloat16 [4096, 3584], P(('blk', 'dp'))
- grad_gate: bfloat16 [16, 3584, 512], P('blk', 'dp')
- grad_up: bfloat16 [16, 3584, 512], P('blk', 'dp')
- grad_down: bfloat16 [16, 3584, 512], P('blk', 'dp')
Inputs may be any that keep to these rules, and one draw needn't show every extreme that they name: A token on blk index b sends its row to expert e = (b // 2 + route_dir - 1) mod 8, whose halves sit at blk indices 2e and 2e + 1; on one device at most 64 tokens take the same value.
All inputs are finite; a program needn't handle non-finite values.
Results may differ from a plain program's by a relative error of at most 0.0079.
Values may be sent and summed in bfloat16 or wider, within the bound.
A program may use at most 128 MiB of HBM per device.

v0:
```python
import functools

import jax
import jax.numpy as jnp
from jax import lax
from jax.experimental import pallas as pl
from jax.experimental.pallas import tpu as pltpu
from jax.sharding import PartitionSpec as P

CAP = 64
TILE = 256
MESH = pl.DeviceIdType.MESH
F32, BF16 = jnp.float32, jnp.bfloat16


def dot(left_side, right_side, left_dim, right_dim):
    return lax.dot_general(
        left_side, right_side, (((left_dim,), (right_dim,)), ((), ())), preferred_element_type=F32
    )


def places_of(chosen):
    tokens = chosen.shape[1]
    before = lax.broadcasted_iota(jnp.int32, (tokens, tokens), 0)
    after = lax.broadcasted_iota(jnp.int32, (tokens, tokens), 1)
    return dot(chosen.astype(BF16), (before <= after).astype(BF16), 1, 0) - 1.0


def slots_of(chosen_row, place_row):
    tokens = chosen_row.shape[1]
    key = jnp.where(chosen_row, place_row, -1.0)
    slot = lax.broadcasted_iota(jnp.int32, (CAP, tokens), 0).astype(F32)
    return slot == jnp.broadcast_to(key, (CAP, tokens))


def kernel(
    n_blk,
    tok, route, probs, w_gate, w_up, w_down,
    out_tok, out_gate, out_up, out_down,
    wg, wu, wd, near_tok, far_tok, facts, sel, outbox, rows,
    pre, pre_send, pre_recv, hid, o_send, o_recv, back, gcol,
    dh, dh_send, dh_recv, dgate, dup, dx_part, dx_recv, dx_sum, home,
    res_near, res_far, grads,
    load_sem, tok_s, tok_r, xf_s, xf_r, ob_s, ob_r, of_s, of_r, side_s, side_r, sf_s, sf_r,
    pre_s, pre_r, o_s, o_r, dh_s, dh_r, dx_s, dx_r, home_s, home_r, res_s, res_r,
    near_sem, grad_sem,
):
    b, d = lax.axis_index("blk"), lax.axis_index("dp")
    c = lax.rem(b, 2)
    other_core = 1 - c
    partner, across = (b + 1 - 2 * c, d), (b, 1 - d)
    upper, lower = (lax.rem(b + 2, n_blk), d), (lax.rem(b + n_blk - 2, n_blk), d)
    wide = near_tok.shape[1]
    hidden = wg.shape[1]
    mine = pl.ds(pl.multiple_of(d * wide, 128), wide)
    theirs = pl.ds(pl.multiple_of((1 - d) * wide, 128), wide)

    def remote(src, dst, ssem, rsem, device):
        return pltpu.make_async_remote_copy(
            src_ref=src, dst_ref=dst, send_sem=ssem, recv_sem=rsem,
            device_id=device, device_id_type=MESH,
        )

    loads = [
        pltpu.make_async_copy(tok.at[:, mine], near_tok, load_sem.at[0]),
        pltpu.make_async_copy(w_gate, wg, load_sem.at[1]),
        pltpu.make_async_copy(w_up, wu, load_sem.at[2]),
        pltpu.make_async_copy(w_down, wd, load_sem.at[3]),
    ]
    for load in loads:
        load.start()

    barrier = pltpu.get_barrier_semaphore()
    for device in (partner, across, upper, lower):
        pl.semaphore_signal(barrier, inc=1, device_id=device, device_id_type=MESH)
    pl.semaphore_wait(barrier, 4)

    x_tok = remote(tok.at[:, theirs], far_tok, tok_s, tok_r, across)
    x_facts = remote(facts.at[0, 1, c], facts.at[1, 1, c], xf_s, xf_r, across)

    def out_rows(g, k):
        return remote(
            outbox.at[g, k], rows.at[g, 2 * k, c], ob_s.at[g, k], ob_r.at[g, k], (lower, upper)[k]
        )

    def out_facts(g, k):
        return remote(
            facts.at[g, 1, c], facts.at[g, 2 * k, c], of_s.at[g, k], of_r.at[g, k],
            (lower, upper)[k],
        )

    def side_rows(g, j):
        return remote(
            rows.at[g, j, c], rows.at[g, j, c], side_s.at[g, j], side_r.at[g, j], partner
        )

    def side_facts(g, j):
        return remote(facts.at[g, j, c], facts.at[g, j, c], sf_s.at[g, j], sf_r.at[g, j], partner)

    def side_rows_in(g, j):
        return remote(
            rows.at[g, j, other_core], rows.at[g, j, other_core],
            side_s.at[g, j], side_r.at[g, j], partner,
        )

    def side_facts_in(g, j):
        return remote(
            facts.at[g, j, other_core], facts.at[g, j, other_core],
            sf_s.at[g, j], sf_r.at[g, j], partner,
        )

    def x_pre(g, j):
        return remote(
            pre_send.at[g, j], pre_recv.at[1 - g, j], pre_s.at[g, j], pre_r.at[1 - g, j], across
        )

    def o_copy(g, j):
        return remote(o_send.at[g, j], o_recv.at[g, j], o_s.at[g, j], o_r.at[g, j], partner)

    def x_dh(g, j):
        return remote(
            dh_send.at[g, j], dh_recv.at[1 - g, j], dh_s.at[g, j], dh_r.at[1 - g, j], across
        )

    def dx_copy(g, j):
        return remote(
            dx_part.at[g, j, other_core], dx_recv.at[g, j], dx_s.at[g, j], dx_r.at[g, j], partner
        )

    def home_copy(g, k):
        return remote(
            dx_sum.at[g, 2 * k], home.at[g, 2 * k], home_s.at[g, k], home_r.at[g, k],
            (upper, lower)[k],
        )

    x_res = remote(res_far, out_tok.at[:, mine], res_s, res_r, across)

    def choose(g):
        fact = facts[g, 1, c]
        kinds = lax.broadcasted_iota(jnp.int32, fact.shape, 0).astype(F32)
        chosen = jnp.broadcast_to(fact[0:1], fact.shape) == kinds
        place = places_of(chosen.astype(F32))
        kept = jnp.where(chosen, place, -1.0)
        slot = lax.broadcasted_iota(jnp.int32, (CAP, fact.shape[1]), 0).astype(F32)
        for j in range(3):
            key = jnp.broadcast_to(kept[j : j + 1], (CAP, fact.shape[1]))
            sel[g, j] = (slot == key).astype(F32).astype(BF16)

    def pick(g, j, source, target):
        target[...] = dot(sel[g, j], source[...], 1, 0).astype(BF16)

    def front(g, source):
        choose(g)
        pick(g, 0, source, outbox.at[g, 0])
        out_rows(g, 0).start()
        pick(g, 2, source, outbox.at[g, 1])
        out_rows(g, 1).start()
        pick(g, 1, source, rows.at[g, 1, c])
        side_rows(g, 1).start()
        for k in range(2):
            out_facts(g, k).start()
        side_facts(g, 1).start()

    x_tok.start()
    pad = jnp.zeros((facts.shape[3] - 2, facts.shape[4]), F32)
    facts[0, 1, c] = jnp.concatenate([route[...].astype(F32), probs[...], pad], axis=0)
    x_facts.start()
    loads[0].wait()
    front(0, near_tok)
    loads[1].wait()
    loads[2].wait()

    @pl.loop(0, 6)
    def _(u):
        g, i = u // 3, u % 3
        j = (1 + 2 * i) % 3

        @pl.when(u == 1)
        def _():
            x_facts.wait_recv()
            x_tok.wait_recv()
            front(1, far_tok)

        @pl.when(i == 1)
        def _():
            for k in range(2):
                out_rows(g, k).wait_recv()
                side_rows(g, 2 * k).start()
            for k in range(2):
                out_facts(g, k).wait_recv()
                side_facts(g, 2 * k).start()

        side_rows_in(g, j).wait_recv()
        unit = rows[g, j].reshape(2 * CAP, wide)
        for part, weight in enumerate((wg, wu)):
            cols = pl.ds(part * hidden, hidden)
            value = dot(unit, weight[...], 1, 0)
            pre[g, j, :, cols] = value
            pre_send[g, j, :, cols] = value.astype(BF16)

        @pl.when(g == 0)
        def _():
            x_pre(g, j).start()

        @pl.when(u == 4)
        def _():
            x_pre(1, 0).start()

        @pl.when(u == 5)
        def _():
            x_pre(1, 2).start()
            x_pre(1, 1).start()

    loads[3].wait()

    def activate(g, j):
        x_pre(1 - g, j).wait_recv()
        full = pre[g, j] + pre_recv[g, j].astype(F32)
        pre[g, j] = full
        gate, up = full[:, :hidden], full[:, hidden:]
        act = (gate * jax.nn.sigmoid(gate) * up).astype(BF16)
        hid[g, j] = act
        o_send[g, j] = dot(act, wd[...], 1, 1).astype(BF16)
        o_copy(g, j).start()

    def back_unit(g, j):
        side_facts_in(g, j).wait_recv()
        for s in range(2):
            fact = facts[g, j, s]
            chosen = jnp.broadcast_to(fact[0:1], fact.shape) == j.astype(F32)
            place = places_of(chosen.astype(F32))
            slots = slots_of(chosen[0:1], place[0:1])
            weight = jnp.where(slots, jnp.broadcast_to(fact[1:2], slots.shape), 0.0)
            gcol[g, j, s] = jnp.broadcast_to(
                jnp.sum(weight, axis=1, keepdims=True), gcol.shape[3:]
            )
        o_copy(g, j).wait_recv()
        gates = gcol[g, j].reshape(2 * CAP, gcol.shape[4])[:, 0:1]
        total = (o_send[g, j].astype(F32) + o_recv[g, j].astype(F32)).astype(BF16)
        rows_back = (gates * (gates * total.astype(F32))).astype(BF16)
        back[g, j] = rows_back
        value = dot(rows_back, wd[...], 1, 0)
        dh[g, j] = value
        dh_send[g, j] = value.astype(BF16)

        @pl.when(g == 0)
        def _():
            x_dh(g, j).start()

    def unit_of(t):
        g = 1 - t // 3
        return g, (2 * (t % 3) + g) % 3

    @pl.loop(0, 7)
    def _(t):
        @pl.when(t < 3)
        def _():
            activate(*unit_of(t))

        @pl.when(t > 0)
        def _():
            back_unit(*unit_of(t - 1))

        @pl.when((t > 2) & (t < 6))
        def _():
            activate(*unit_of(t))

    for j in (0, 2, 1):
        x_dh(1, j).start()

    def grad_unit(k, left, right, target):
        @pl.loop(0, wide // TILE)
        def _(n):
            cols = pl.ds(pl.multiple_of(n * TILE, TILE), TILE)
            value = dot(
                left[..., cols].reshape(-1, TILE), right[...].reshape(-1, hidden), 0, 0
            )
            grads[k, cols, :] = value.astype(BF16)
            pltpu.make_async_copy(
                grads.at[k, cols, :], target.at[cols, :], grad_sem.at[k, n]
            ).start()

    def down_unit(g, j):
        x_dh(1 - g, j).wait_recv()
        d_hidden = dh[g, j] + dh_recv[g, j].astype(F32)
        gate, up = pre[g, j, :, :hidden], pre[g, j, :, hidden:]
        sigmoid = jax.nn.sigmoid(gate)
        d_g = (d_hidden * up * (sigmoid * (1.0 + gate * (1.0 - sigmoid)))).astype(BF16)
        d_u = (d_hidden * (gate * sigmoid)).astype(BF16)
        dgate[g, j] = d_g
        dup[g, j] = d_u
        value = dot(d_g, wg[...], 1, 1) + dot(d_u, wu[...], 1, 1)
        dx_part[g, j] = value.astype(BF16).reshape(2, CAP, wide)
        dx_copy(g, j).start()

    def join_unit(g, j):
        dx_copy(g, j).wait_recv()
        dx_sum[g, j] = (dx_part[g, j, c].astype(F32) + dx_recv[g, j].astype(F32)).astype(BF16)

        @pl.when(j == 0)
        def _():
            home_copy(g, 0).start()

        @pl.when(j == 2)
        def _():
            home_copy(g, 1).start()

        @pl.when(j == 1)
        def _():
            home[g, j] = dx_sum[g, j]

    def unpack(g, target):
        for k in range(2):
            home_copy(g, k).wait_recv()
        tokens = sel.shape[3]
        target[...] = dot(
            sel[g].reshape(3 * CAP, tokens), home[g].reshape(3 * CAP, wide), 0, 0
        ).astype(BF16)

    def last_of(t):
        return 1 - t // 3, (2 * (t % 3)) % 3

    @pl.loop(0, 7)
    def _(t):
        @pl.when(t > 0)
        def _():
            join_unit(*last_of(t - 1))

        @pl.when(t == 3)
        def _():
            grad_unit(2, back, hid, out_down)

        @pl.when(t == 4)
        def _():
            unpack(1, res_far)
            x_res.start()

        @pl.when(t < 6)
        def _():
            down_unit(*last_of(t))

    grad_unit(0, rows, dgate, out_gate)
    grad_unit(1, rows, dup, out_up)
    unpack(0, res_near)
    near_out = pltpu.make_async_copy(res_near, out_tok.at[:, mine], near_sem)
    near_out.start()

    x_tok.wait_send()
    x_facts.wait_send()
    for g in range(2):
        for k in range(2):
            out_rows(g, k).wait_send()
            out_facts(g, k).wait_send()
            home_copy(g, k).wait_send()
        for j in range(3):
            side_rows(g, j).wait_send()
            side_facts(g, j).wait_send()
            x_pre(g, j).wait_send()
            o_copy(g, j).wait_send()
            x_dh(g, j).wait_send()
            dx_copy(g, j).wait_send()
    for k, target in enumerate((out_gate, out_up, out_down)):
        for n in range(wide // TILE):
            cols = pl.ds(n * TILE, TILE)
            pltpu.make_async_copy(
                grads.at[k, cols, :], target.at[cols, :], grad_sem.at[k, n]
            ).wait()
    near_out.wait()
    x_res.wait_send()
    remote(res_far, out_tok.at[:, theirs], res_s, res_r, across).wait_recv()


def per_device(n_blk, tokens, route_dir, gate_probs, gate_weight, up_weight, down_weight):
    count, model = tokens.shape
    _, wide, hidden = gate_weight.shape
    dma = pltpu.SemaphoreType.DMA
    vmem = pltpu.VMEM
    units = 2 * CAP
    outs = pl.pallas_call(
        functools.partial(kernel, n_blk),
        out_shape=(
            jax.ShapeDtypeStruct((count, model), BF16),
            jax.ShapeDtypeStruct((wide, hidden), BF16),
            jax.ShapeDtypeStruct((wide, hidden), BF16),
            jax.ShapeDtypeStruct((wide, hidden), BF16),
        ),
        in_specs=[
            pl.BlockSpec(memory_space=pl.ANY),
            pl.BlockSpec(memory_space=pltpu.VMEM),
            pl.BlockSpec(memory_space=pltpu.VMEM),
            pl.BlockSpec(memory_space=pl.ANY),
            pl.BlockSpec(memory_space=pl.ANY),
            pl.BlockSpec(memory_space=pl.ANY),
        ],
        out_specs=[pl.BlockSpec(memory_space=pl.ANY)] * 4,
        scratch_shapes=[
            vmem((wide, hidden), BF16),
            vmem((wide, hidden), BF16),
            vmem((wide, hidden), BF16),
            vmem((count, wide), BF16),
            vmem((count, wide), BF16),
            vmem((2, 3, 2, 8, count), F32),
            vmem((2, 3, CAP, count), BF16),
            vmem((2, 2, CAP, wide), BF16),
            vmem((2, 3, 2, CAP, wide), BF16),
            vmem((2, 3, units, 2 * hidden), F32),
            vmem((2, 3, units, 2 * hidden), BF16),
            vmem((2, 3, units, 2 * hidden), BF16),
            vmem((2, 3, units, hidden), BF16),
            vmem((2, 3, units, wide), BF16),
            vmem((2, 3, units, wide), BF16),
            vmem((2, 3, units, wide), BF16),
            vmem((2, 3, 2, CAP, 128), F32),
            vmem((2, 3, units, hidden), F32),
            vmem((2, 3, units, hidden), BF16),
            vmem((2, 3, units, hidden), BF16),
            vmem((2, 3, units, hidden), BF16),
            vmem((2, 3, units, hidden), BF16),
            vmem((2, 3, 2, CAP, wide), BF16),
            vmem((2, 3, CAP, wide), BF16),
            vmem((2, 3, CAP, wide), BF16),
            vmem((2, 3, CAP, wide), BF16),
            vmem((count, wide), BF16),
            vmem((count, wide), BF16),
            vmem((3, wide, hidden), BF16),
            dma((4,)),
            dma, dma, dma, dma,
            dma((2, 2)), dma((2, 2)), dma((2, 2)), dma((2, 2)),
            dma((2, 3)), dma((2, 3)), dma((2, 3)), dma((2, 3)),
            dma((2, 3)), dma((2, 3)), dma((2, 3)), dma((2, 3)),
            dma((2, 3)), dma((2, 3)), dma((2, 3)), dma((2, 3)),
            dma((2, 2)), dma((2, 2)),
            dma, dma,
            dma,
            dma((3, wide // TILE)),
        ],
        compiler_params=pltpu.CompilerParams(
            collective_id=0, has_side_effects=True, vmem_limit_bytes=60 << 20
        ),
    )(
        tokens,
        route_dir.reshape(1, count),
        gate_probs.reshape(1, count),
        gate_weight[0],
        up_weight[0],
        down_weight[0],
    )
    d_tokens, grad_gate, grad_up, grad_down = outs
    return d_tokens, grad_gate[None], grad_up[None], grad_down[None]


def solution(mesh):
    return jax.shard_map(
        functools.partial(per_device, mesh.shape["blk"]),
        mesh=mesh,
        in_specs=(
            P(("blk", "dp"), None),
            P(("blk", "dp"), None),
            P(("blk", "dp"), None),
            P("blk", "dp", None),
            P("blk", "dp", None),
            P("blk", "dp", None),
        ),
        out_specs=(
            P(("blk", "dp"), None),
            P("blk", "dp", None),
            P("blk", "dp", None),
            P("blk", "dp", None),
        ),
        check_vma=False,
    )
```

profile of v0, /device:TPU:0, one launch (start us, length us, event | category | flops | bytes accessed | tf_op | source)
XLA Modules:
  0.0 91.9 jit_solution(12878766636365358089)
XLA Ops:
  0.6 83.4 %shard_map.93 = (bf16[128,3584]{1,0:T(8,128)(2,1)}, bf16[1792,512]{1,0:T(8,128)(2,1)}, bf16[1792,512]{1,0:T(8,128)(2,1)}, bf16[1792,512]{1,0:T(8,128)(2,1)}) custom-call(bf16[128,3584]{1,0:T(8,128)(2,1)} %tok.1, s32[1,128]{1,0:T(1,128)} %bitcast.14, f32[1,128]{1,0:T(1,128)} %bitcast.15, bf16[1792,512]{1,0:T(8,128)(2,1)} %bitcast.11, ...), custom_call_target="tpu_custom_call" | custom-call | tf_op jit(solution)/shard_map/pallas_call | solution.py:379
  84.1 0.0 copy-start.2
  84.1 2.3 %copy.14 = bf16[128,3584]{1,0:T(8,128)(2,1)} copy(bf16[128,3584]{1,0:T(8,128)(2,1)} %get-tuple-element.16) | data formatting | bytes 1835008
  86.4 0.0 copy-done.2
  86.4 0.0 copy-start.1
  86.4 1.2 %copy.15 = bf16[1,1792,512]{2,1,0:T(8,128)(2,1)} copy(bf16[1,1792,512]{2,1,0:T(8,128)(2,1)S(1)} %bitcast.10) | data formatting | bytes 3670016
  87.6 0.9 %copy-done.1 = bf16[1792,512]{1,0:T(8,128)(2,1)S(1)} copy-done((bf16[1792,512]{1,0:T(8,128)(2,1)S(1)}, bf16[1792,512]{1,0:T(8,128)(2,1)}, u32[]{:S(2)}) %copy-start.1) | copy-done | bytes 1835032
  88.5 0.0 copy-start
  88.5 1.2 %copy.16 = bf16[1,1792,512]{2,1,0:T(8,128)(2,1)} copy(bf16[1,1792,512]{2,1,0:T(8,128)(2,1)S(1)} %bitcast.9) | data formatting | bytes 3670016
  89.8 0.9 %copy-done = bf16[1792,512]{1,0:T(8,128)(2,1)S(1)} copy-done((bf16[1792,512]{1,0:T(8,128)(2,1)S(1)}, bf16[1792,512]{1,0:T(8,128)(2,1)}, u32[]{:S(2)}) %copy-start) | copy-done | bytes 1835032
  90.7 1.2 %copy.17 = bf16[1,1792,512]{2,1,0:T(8,128)(2,1)} copy(bf16[1,1792,512]{2,1,0:T(8,128)(2,1)S(1)} %bitcast.8) | data formatting | bytes 3670016
Async XLA Ops:
  84.1 2.3 %copy-start.2 = (bf16[1792,512]{1,0:T(8,128)(2,1)S(1)}, bf16[1792,512]{1,0:T(8,128)(2,1)}, u32[]{:S(2)}) copy-start(bf16[1792,512]{1,0:T(8,128)(2,1)} %get-tuple-element.9) | copy-start | bytes 5505028
  86.4 2.2 %copy-start.1 = (bf16[1792,512]{1,0:T(8,128)(2,1)S(1)}, bf16[1792,512]{1,0:T(8,128)(2,1)}, u32[]{:S(2)}) copy-start(bf16[1792,512]{1,0:T(8,128)(2,1)} %get-tuple-element.10) | copy-start | bytes 5505028
  88.5 2.2 %copy-start = (bf16[1792,512]{1,0:T(8,128)(2,1)S(1)}, bf16[1792,512]{1,0:T(8,128)(2,1)}, u32[]{:S(2)}) copy-start(bf16[1792,512]{1,0:T(8,128)(2,1)} %get-tuple-element.11) | copy-start | bytes 5505028
where the time goes:
time: 92.2 us; the launch traced here: 91.9 us
  Pallas kernels  83.4 us (90%)
  local copies, waits for them, and re-layouts  7.85 us (9%)
    pallas_call x1, Pallas kernels, per_device(): pl.pallas_call(functools.partial(kernel, n_blk), out_shape=(jax.ShapeDtyp...  83.4 us
    unnamed x10, local copies, waits for them, and re-layouts  7.85 us

commit v1 on v0

--- a/solution.py
+++ b/solution.py
@@ -8,7 +8,7 @@
 from jax.sharding import PartitionSpec as P
 
 CAP = 64
-TILE = 256
+GRAD_PARTS = 2
 MESH = pl.DeviceIdType.MESH
 F32, BF16 = jnp.float32, jnp.bfloat16
 
@@ -35,9 +35,9 @@
 
 def kernel(
     n_blk,
-    tok, route, probs, w_gate, w_up, w_down,
+    tok, route_in, probs_in, w_gate, w_up, w_down,
     out_tok, out_gate, out_up, out_down,
-    wg, wu, wd, near_tok, far_tok, facts, sel, outbox, rows,
+    route, probs, wg, wu, wd, near_tok, far_tok, facts, sel, outbox, rows,
     pre, pre_send, pre_recv, hid, o_send, o_recv, back, gcol,
     dh, dh_send, dh_recv, dgate, dup, dx_part, dx_recv, dx_sum, home,
     res_near, res_far, grads,
@@ -52,6 +52,7 @@
     upper, lower = (lax.rem(b + 2, n_blk), d), (lax.rem(b + n_blk - 2, n_blk), d)
     wide = near_tok.shape[1]
     hidden = wg.shape[1]
+    tile = wide // GRAD_PARTS
     mine = pl.ds(pl.multiple_of(d * wide, 128), wide)
     theirs = pl.ds(pl.multiple_of((1 - d) * wide, 128), wide)
 
@@ -62,6 +63,8 @@
         )
 
     loads = [
+        pltpu.make_async_copy(route_in, route, load_sem.at[4]),
+        pltpu.make_async_copy(probs_in, probs, load_sem.at[5]),
         pltpu.make_async_copy(tok.at[:, mine], near_tok, load_sem.at[0]),
         pltpu.make_async_copy(w_gate, wg, load_sem.at[1]),
         pltpu.make_async_copy(w_up, wu, load_sem.at[2]),
@@ -163,33 +166,22 @@
 
     x_tok.start()
     pad = jnp.zeros((facts.shape[3] - 2, facts.shape[4]), F32)
+    loads[0].wait()
+    loads[1].wait()
     facts[0, 1, c] = jnp.concatenate([route[...].astype(F32), probs[...], pad], axis=0)
     x_facts.start()
-    loads[0].wait()
+    loads[2].wait()
     front(0, near_tok)
-    loads[1].wait()
-    loads[2].wait()
-
-    @pl.loop(0, 6)
-    def _(u):
-        g, i = u // 3, u % 3
-        j = (1 + 2 * i) % 3
-
-        @pl.when(u == 1)
-        def _():
-            x_facts.wait_recv()
-            x_tok.wait_recv()
-            front(1, far_tok)
-
-        @pl.when(i == 1)
-        def _():
-            for k in range(2):
-                out_rows(g, k).wait_recv()
-                side_rows(g, 2 * k).start()
-            for k in range(2):
-                out_facts(g, k).wait_recv()
-                side_facts(g, 2 * k).start()
-
+    loads[3].wait()
+    loads[4].wait()
+
+    def forward(g, k):
+        out_rows(g, k).wait_recv()
+        side_rows(g, 2 * k).start()
+        out_facts(g, k).wait_recv()
+        side_facts(g, 2 * k).start()
+
+    def first(g, j):
         side_rows_in(g, j).wait_recv()
         unit = rows[g, j].reshape(2 * CAP, wide)
         for part, weight in enumerate((wg, wu)):
@@ -197,21 +189,6 @@
             value = dot(unit, weight[...], 1, 0)
             pre[g, j, :, cols] = value
             pre_send[g, j, :, cols] = value.astype(BF16)
-
-        @pl.when(g == 0)
-        def _():
-            x_pre(g, j).start()
-
-        @pl.when(u == 4)
-        def _():
-            x_pre(1, 0).start()
-
-        @pl.when(u == 5)
-        def _():
-            x_pre(1, 2).start()
-            x_pre(1, 1).start()
-
-    loads[3].wait()
 
     def activate(g, j):
         x_pre(1 - g, j).wait_recv()
@@ -227,7 +204,7 @@
         side_facts_in(g, j).wait_recv()
         for s in range(2):
             fact = facts[g, j, s]
-            chosen = jnp.broadcast_to(fact[0:1], fact.shape) == j.astype(F32)
+            chosen = jnp.broadcast_to(fact[0:1], fact.shape) == float(j)
             place = places_of(chosen.astype(F32))
             slots = slots_of(chosen[0:1], place[0:1])
             weight = jnp.where(slots, jnp.broadcast_to(fact[1:2], slots.shape), 0.0)
@@ -243,37 +220,11 @@
         dh[g, j] = value
         dh_send[g, j] = value.astype(BF16)
 
-        @pl.when(g == 0)
-        def _():
-            x_dh(g, j).start()
-
-    def unit_of(t):
-        g = 1 - t // 3
-        return g, (2 * (t % 3) + g) % 3
-
-    @pl.loop(0, 7)
-    def _(t):
-        @pl.when(t < 3)
-        def _():
-            activate(*unit_of(t))
-
-        @pl.when(t > 0)
-        def _():
-            back_unit(*unit_of(t - 1))
-
-        @pl.when((t > 2) & (t < 6))
-        def _():
-            activate(*unit_of(t))
-
-    for j in (0, 2, 1):
-        x_dh(1, j).start()
-
     def grad_unit(k, left, right, target):
-        @pl.loop(0, wide // TILE)
-        def _(n):
-            cols = pl.ds(pl.multiple_of(n * TILE, TILE), TILE)
+        for n in range(wide // tile):
+            cols = pl.ds(n * tile, tile)
             value = dot(
-                left[..., cols].reshape(-1, TILE), right[...].reshape(-1, hidden), 0, 0
+                left[..., cols].reshape(-1, tile), right[...].reshape(-1, hidden), 0, 0
             )
             grads[k, cols, :] = value.astype(BF16)
             pltpu.make_async_copy(
@@ -297,17 +248,10 @@
         dx_copy(g, j).wait_recv()
         dx_sum[g, j] = (dx_part[g, j, c].astype(F32) + dx_recv[g, j].astype(F32)).astype(BF16)
 
-        @pl.when(j == 0)
-        def _():
-            home_copy(g, 0).start()
-
-        @pl.when(j == 2)
-        def _():
-            home_copy(g, 1).start()
-
-        @pl.when(j == 1)
-        def _():
+        if j == 1:
             home[g, j] = dx_sum[g, j]
+        else:
+            home_copy(g, j // 2).start()
 
     def unpack(g, target):
         for k in range(2):
@@ -317,28 +261,59 @@
             sel[g].reshape(3 * CAP, tokens), home[g].reshape(3 * CAP, wide), 0, 0
         ).astype(BF16)
 
-    def last_of(t):
-        return 1 - t // 3, (2 * (t % 3)) % 3
-
-    @pl.loop(0, 7)
-    def _(t):
-        @pl.when(t > 0)
-        def _():
-            join_unit(*last_of(t - 1))
-
-        @pl.when(t == 3)
-        def _():
-            grad_unit(2, back, hid, out_down)
-
-        @pl.when(t == 4)
-        def _():
-            unpack(1, res_far)
-            x_res.start()
-
-        @pl.when(t < 6)
-        def _():
-            down_unit(*last_of(t))
-
+    first(0, 1)
+    x_pre(0, 1).start()
+    x_facts.wait_recv()
+    x_tok.wait_recv()
+    front(1, far_tok)
+    for k in range(2):
+        forward(0, k)
+    for j in (0, 2):
+        first(0, j)
+        x_pre(0, j).start()
+    first(1, 1)
+    for k in range(2):
+        forward(1, k)
+    for j in (0, 2):
+        first(1, j)
+        x_pre(1, j).start()
+    loads[5].wait()
+
+    activate(1, 1)
+    activate(1, 0)
+    back_unit(1, 1)
+    activate(1, 2)
+    back_unit(1, 0)
+    back_unit(1, 2)
+
+    activate(0, 0)
+    back_unit(0, 0)
+    x_dh(0, 0).start()
+    x_pre(1, 1).start()
+    activate(0, 2)
+    back_unit(0, 2)
+    x_dh(0, 2).start()
+    x_dh(1, 0).start()
+    x_dh(1, 2).start()
+    down_unit(1, 0)
+    join_unit(1, 0)
+    activate(0, 1)
+    back_unit(0, 1)
+    x_dh(0, 1).start()
+    x_dh(1, 1).start()
+    down_unit(1, 2)
+    join_unit(1, 2)
+    down_unit(0, 0)
+    down_unit(1, 1)
+    join_unit(0, 0)
+    join_unit(1, 1)
+    unpack(1, res_far)
+    x_res.start()
+    down_unit(0, 2)
+    down_unit(0, 1)
+    join_unit(0, 2)
+    join_unit(0, 1)
+    grad_unit(2, back, hid, out_down)
     grad_unit(0, rows, dgate, out_gate)
     grad_unit(1, rows, dup, out_up)
     unpack(0, res_near)
@@ -360,14 +335,48 @@
             x_dh(g, j).wait_send()
             dx_copy(g, j).wait_send()
     for k, target in enumerate((out_gate, out_up, out_down)):
-        for n in range(wide // TILE):
-            cols = pl.ds(n * TILE, TILE)
+        for n in range(wide // tile):
+            cols = pl.ds(n * tile, tile)
             pltpu.make_async_copy(
                 grads.at[k, cols, :], target.at[cols, :], grad_sem.at[k, n]
             ).wait()
     near_out.wait()
     x_res.wait_send()
     remote(res_far, out_tok.at[:, theirs], res_s, res_r, across).wait_recv()
+
+
+def settle_kernel(parts, *refs):
+    count = len(refs) // 2
+    sources, targets, sem = refs[:count], refs[count : 2 * count], refs[-1]
+    copies = []
+    for k in range(count):
+        rows = sources[k].shape[0] // parts
+        for part in range(parts):
+            span = pl.ds(part * rows, rows)
+            copies.append(
+                pltpu.make_async_copy(
+                    sources[k].at[span, :], targets[k].at[span, :], sem.at[k, part]
+                )
+            )
+    for copy in copies:
+        copy.start()
+    for copy in copies:
+        copy.wait()
+
+
+def settled(arrays, parts=4):
+    return pl.pallas_call(
+        functools.partial(settle_kernel, parts),
+        out_shape=tuple(jax.ShapeDtypeStruct(a.shape, a.dtype) for a in arrays),
+        in_specs=[pl.BlockSpec(memory_space=pl.ANY)] * len(arrays),
+        out_specs=[pl.BlockSpec(memory_space=pltpu.HBM)] * len(arrays),
+        scratch_shapes=[pltpu.SemaphoreType.DMA((len(arrays), parts))],
+        compiler_params=pltpu.CompilerParams(vmem_limit_bytes=1 << 20),
+    )(*arrays)
+
+
+def in_hbm(array):
+    return pltpu.with_memory_space_constraint(array, pltpu.HBM)
 
 
 def per_device(n_blk, tokens, route_dir, gate_probs, gate_weight, up_weight, down_weight):
@@ -385,15 +394,17 @@
             jax.ShapeDtypeStruct((wide, hidden), BF16),
         ),
         in_specs=[
-            pl.BlockSpec(memory_space=pl.ANY),
-            pl.BlockSpec(memory_space=pltpu.VMEM),
-            pl.BlockSpec(memory_space=pltpu.VMEM),
-            pl.BlockSpec(memory_space=pl.ANY),
-            pl.BlockSpec(memory_space=pl.ANY),
-            pl.BlockSpec(memory_space=pl.ANY),
+            pl.BlockSpec(memory_space=pltpu.HBM),
+            pl.BlockSpec(memory_space=pltpu.HBM),
+            pl.BlockSpec(memory_space=pltpu.HBM),
+            pl.BlockSpec(memory_space=pltpu.HBM),
+            pl.BlockSpec(memory_space=pltpu.HBM),
+            pl.BlockSpec(memory_space=pltpu.HBM),
         ],
         out_specs=[pl.BlockSpec(memory_space=pl.ANY)] * 4,
         scratch_shapes=[
+            vmem((1, count), jnp.int32),
+            vmem((1, count), F32),
             vmem((wide, hidden), BF16),
             vmem((wide, hidden), BF16),
             vmem((wide, hidden), BF16),
@@ -423,7 +434,7 @@
             vmem((count, wide), BF16),
             vmem((count, wide), BF16),
             vmem((3, wide, hidden), BF16),
-            dma((4,)),
+            dma((6,)),
             dma, dma, dma, dma,
             dma((2, 2)), dma((2, 2)), dma((2, 2)), dma((2, 2)),
             dma((2, 3)), dma((2, 3)), dma((2, 3)), dma((2, 3)),
@@ -432,20 +443,20 @@
             dma((2, 2)), dma((2, 2)),
             dma, dma,
             dma,
-            dma((3, wide // TILE)),
+            dma((3, GRAD_PARTS)),
         ],
         compiler_params=pltpu.CompilerParams(
-            collective_id=0, has_side_effects=True, vmem_limit_bytes=60 << 20
+            collective_id=0, has_side_effects=True, vmem_limit_bytes=46 << 20
         ),
     )(
-        tokens,
-        route_dir.reshape(1, count),
-        gate_probs.reshape(1, count),
-        gate_weight[0],
-        up_weight[0],
-        down_weight[0],
+        in_hbm(tokens),
+        in_hbm(route_dir.reshape(1, count)),
+        in_hbm(gate_probs.reshape(1, count)),
+        in_hbm(gate_weight[0]),
+        in_hbm(up_weight[0]),
+        in_hbm(down_weight[0]),
     )
-    d_tokens, grad_gate, grad_up, grad_down = outs
+    d_tokens, grad_gate, grad_up, grad_down = settled(outs)
     return d_tokens, grad_gate[None], grad_up[None], grad_down[None]
 
 

time: 92.2 us -> 85.8 us (0.931)
  local copies, waits for them, and re-layouts: 7.85 us -> 0 us
  Pallas kernels: 83.4 us -> 84.9 us
    unnamed x10 -> x0, local copies, waits for them, and re-layouts: 7.85 us -> none
    pallas_call x0 -> x1, Pallas kernels: none -> 2.83 us  [settled(): pl.pallas_call(functools.partial(settle_kernel, parts), out_shape=tuple((...]
    pallas_call x1, Pallas kernels: 83.4 us -> 82 us  [per_device(): pl.pallas_call(functools.partial(kernel, n_blk), out_shape=(jax.ShapeDtyp...]
where the time goes in v1:
time: 85.8 us; the launch traced here: 85.7 us
  Pallas kernels  84.9 us (99%)
    pallas_call x1, Pallas kernels, per_device(): pl.pallas_call(functools.partial(kernel, n_blk), out_shape=(jax.ShapeDtyp...  82 us
    pallas_call x1, Pallas kernels, settled(): pl.pallas_call(functools.partial(settle_kernel, parts), out_shape=tuple((...  2.83 us

profile of v1, /device:TPU:0, one launch (start us, length us, event | category | flops | bytes accessed | tf_op | source)
XLA Modules:
  0.0 85.7 jit_solution(15018305158074497905)
XLA Ops:
  0.6 82.0 %shard_map.93 = (bf16[128,3584]{1,0:T(8,128)(2,1)S(1)}, bf16[1792,512]{1,0:T(8,128)(2,1)S(1)}, bf16[1792,512]{1,0:T(8,128)(2,1)S(1)}, bf16[1792,512]{1,0:T(8,128)(2,1)S(1)}) custom-call(bf16[128,3584]{1,0:T(8,128)(2,1)} %tok.1, s32[1,128]{1,0:T(1,128)} %bitcast.11, f32[1,128]{1,0:T(1,128)} %bitcast.12, bf16[1792,512]{1,0:T(8,128)(2,1)} %bitcast.8, ...), custom_call_target="tpu_custom_call" | custom-call | tf_op jit(solution)/shard_map/pallas_call | solution.py:388
  82.7 2.8 %shard_map.94 = (bf16[128,3584]{1,0:T(8,128)(2,1)}, bf16[1792,512]{1,0:T(8,128)(2,1)}, bf16[1792,512]{1,0:T(8,128)(2,1)}, bf16[1792,512]{1,0:T(8,128)(2,1)}) custom-call(bf16[128,3584]{1,0:T(8,128)(2,1)S(1)} %get-tuple-element.12.refs_0_, bf16[1792,512]{1,0:T(8,128)(2,1)S(1)} %get-tuple-element.13.refs_1_, bf16[1792,512]{1,0:T(8,128)(2,1)S(1)} %get-tuple-element.14.refs_2_, ...), custom_call_target="tpu_custom_call" | custom-call | tf_op jit(solution)/shard_map/pallas_call | solution.py:368

commit v2 on v1

--- a/solution.py
+++ b/solution.py
@@ -43,7 +43,7 @@
     res_near, res_far, grads,
     load_sem, tok_s, tok_r, xf_s, xf_r, ob_s, ob_r, of_s, of_r, side_s, side_r, sf_s, sf_r,
     pre_s, pre_r, o_s, o_r, dh_s, dh_r, dx_s, dx_r, home_s, home_r, res_s, res_r,
-    near_sem, grad_sem,
+    near_sem, grad_sem, across_in, cycle_in,
 ):
     b, d = lax.axis_index("blk"), lax.axis_index("dp")
     c = lax.rem(b, 2)
@@ -74,9 +74,34 @@
         load.start()
 
     barrier = pltpu.get_barrier_semaphore()
-    for device in (partner, across, upper, lower):
+    even = b - c
+    greeted = (
+        (even, 1 - d),
+        (lax.rem(even + 2, n_blk) + 1, d),
+        (lax.rem(even + n_blk - 2, n_blk) + 1, d),
+    )
+    for device in greeted:
         pl.semaphore_signal(barrier, inc=1, device_id=device, device_id_type=MESH)
-    pl.semaphore_wait(barrier, 4)
+
+    @pl.when(c == 0)
+    def _():
+        pl.semaphore_wait(barrier, 3)
+        pl.semaphore_signal(across_in, inc=1, device_id=partner, device_id_type=MESH)
+
+    @pl.when(c == 1)
+    def _():
+        pl.semaphore_signal(barrier, inc=1, device_id=partner, device_id_type=MESH)
+        pl.semaphore_wait(across_in, 1)
+
+    def hear_cycle():
+        @pl.when(c == 1)
+        def _():
+            pl.semaphore_wait(barrier, 4)
+            pl.semaphore_signal(cycle_in, inc=1, device_id=partner, device_id_type=MESH)
+
+        @pl.when(c == 0)
+        def _():
+            pl.semaphore_wait(cycle_in, 1)
 
     x_tok = remote(tok.at[:, theirs], far_tok, tok_s, tok_r, across)
     x_facts = remote(facts.at[0, 1, c], facts.at[1, 1, c], xf_s, xf_r, across)
@@ -155,6 +180,8 @@
     def front(g, source):
         choose(g)
         pick(g, 0, source, outbox.at[g, 0])
+        if g == 0:
+            hear_cycle()
         out_rows(g, 0).start()
         pick(g, 2, source, outbox.at[g, 1])
         out_rows(g, 1).start()
@@ -294,21 +321,21 @@
     back_unit(0, 2)
     x_dh(0, 2).start()
     x_dh(1, 0).start()
-    x_dh(1, 2).start()
     down_unit(1, 0)
     join_unit(1, 0)
     activate(0, 1)
     back_unit(0, 1)
     x_dh(0, 1).start()
+    x_dh(1, 2).start()
     x_dh(1, 1).start()
     down_unit(1, 2)
     join_unit(1, 2)
     down_unit(0, 0)
     down_unit(1, 1)
-    join_unit(0, 0)
     join_unit(1, 1)
     unpack(1, res_far)
     x_res.start()
+    join_unit(0, 0)
     down_unit(0, 2)
     down_unit(0, 1)
     join_unit(0, 2)
@@ -444,6 +471,8 @@
             dma, dma,
             dma,
             dma((3, GRAD_PARTS)),
+            pltpu.SemaphoreType.REGULAR,
+            pltpu.SemaphoreType.REGULAR,
         ],
         compiler_params=pltpu.CompilerParams(
             collective_id=0, has_side_effects=True, vmem_limit_bytes=46 << 20

time: 85.8 us -> 84 us (0.979)
  Pallas kernels: 84.9 us -> 83.1 us
    pallas_call x1, Pallas kernels: 82 us -> 80.2 us  [per_device(): pl.pallas_call(functools.partial(kernel, n_blk), out_shape=(jax.ShapeDtyp...]
where the time goes in v2:
time: 84 us; the launch traced here: 83.9 us
  Pallas kernels  83.1 us (99%)
    pallas_call x1, Pallas kernels, per_device(): pl.pallas_call(functools.partial(kernel, n_blk), out_shape=(jax.ShapeDtyp...  80.2 us
    pallas_call x1, Pallas kernels, settled(): pl.pallas_call(functools.partial(settle_kernel, parts), out_shape=tuple((...  2.83 us

profile of v2, /device:TPU:0, one launch (start us, length us, event | category | flops | bytes accessed | tf_op | source)
XLA Modules:
  0.0 83.9 jit_solution(318771995371935019)
XLA Ops:
  0.6 80.2 %shard_map.93 = (bf16[128,3584]{1,0:T(8,128)(2,1)S(1)}, bf16[1792,512]{1,0:T(8,128)(2,1)S(1)}, bf16[1792,512]{1,0:T(8,128)(2,1)S(1)}, bf16[1792,512]{1,0:T(8,128)(2,1)S(1)}) custom-call(bf16[128,3584]{1,0:T(8,128)(2,1)} %tok.1, s32[1,128]{1,0:T(1,128)} %bitcast.11, f32[1,128]{1,0:T(1,128)} %bitcast.12, bf16[1792,512]{1,0:T(8,128)(2,1)} %bitcast.8, ...), custom_call_target="tpu_custom_call" | custom-call | tf_op jit(solution)/shard_map/pallas_call | solution.py:415
  80.9 2.8 %shard_map.94 = (bf16[128,3584]{1,0:T(8,128)(2,1)}, bf16[1792,512]{1,0:T(8,128)(2,1)}, bf16[1792,512]{1,0:T(8,128)(2,1)}, bf16[1792,512]{1,0:T(8,128)(2,1)}) custom-call(bf16[128,3584]{1,0:T(8,128)(2,1)S(1)} %get-tuple-element.12.refs_0_, bf16[1792,512]{1,0:T(8,128)(2,1)S(1)} %get-tuple-element.13.refs_1_, bf16[1792,512]{1,0:T(8,128)(2,1)S(1)} %get-tuple-element.14.refs_2_, ...), custom_call_target="tpu_custom_call" | custom-call | tf_op jit(solution)/shard_map/pallas_call | solution.py:395

commit v3 on v2

--- a/solution.py
+++ b/solution.py
@@ -37,10 +37,10 @@
     n_blk,
     tok, route_in, probs_in, w_gate, w_up, w_down,
     out_tok, out_gate, out_up, out_down,
-    route, probs, wg, wu, wd, near_tok, far_tok, facts, sel, outbox, rows,
+    route, probs, wg, wu, wd, wg_t, wu_t, near_tok, far_tok, facts, sel, outbox, rows,
     pre, pre_send, pre_recv, hid, o_send, o_recv, back, gcol,
-    dh, dh_send, dh_recv, dgate, dup, dx_part, dx_recv, dx_sum, home,
-    res_near, res_far, grads,
+    dh, dh_send, dh_recv, dgu, dx_part, dx_recv, home,
+    res_far, grads,
     load_sem, tok_s, tok_r, xf_s, xf_r, ob_s, ob_r, of_s, of_r, side_s, side_r, sf_s, sf_r,
     pre_s, pre_r, o_s, o_r, dh_s, dh_r, dx_s, dx_r, home_s, home_r, res_s, res_r,
     near_sem, grad_sem, across_in, cycle_in,
@@ -157,7 +157,7 @@
 
     def home_copy(g, k):
         return remote(
-            dx_sum.at[g, 2 * k], home.at[g, 2 * k], home_s.at[g, k], home_r.at[g, k],
+            dx_part.at[g, 2 * k, c], home.at[g, 2 * k], home_s.at[g, k], home_r.at[g, k],
             (upper, lower)[k],
         )
 
@@ -247,16 +247,18 @@
         dh[g, j] = value
         dh_send[g, j] = value.astype(BF16)
 
-    def grad_unit(k, left, right, target):
+    def grad_unit(left, right, targets):
         for n in range(wide // tile):
             cols = pl.ds(n * tile, tile)
             value = dot(
-                left[..., cols].reshape(-1, tile), right[...].reshape(-1, hidden), 0, 0
+                left[..., cols].reshape(-1, tile), right[...].reshape(-1, right.shape[3]), 0, 0
             )
-            grads[k, cols, :] = value.astype(BF16)
-            pltpu.make_async_copy(
-                grads.at[k, cols, :], target.at[cols, :], grad_sem.at[k, n]
-            ).start()
+            for part, (k, target) in enumerate(targets):
+                own = value[:, part * hidden : (part + 1) * hidden]
+                grads[k, cols, :] = own.astype(BF16)
+                pltpu.make_async_copy(
+                    grads.at[k, cols, :], target.at[cols, :], grad_sem.at[k, n]
+                ).start()
 
     def down_unit(g, j):
         x_dh(1 - g, j).wait_recv()
@@ -265,24 +267,28 @@
         sigmoid = jax.nn.sigmoid(gate)
         d_g = (d_hidden * up * (sigmoid * (1.0 + gate * (1.0 - sigmoid)))).astype(BF16)
         d_u = (d_hidden * (gate * sigmoid)).astype(BF16)
-        dgate[g, j] = d_g
-        dup[g, j] = d_u
-        value = dot(d_g, wg[...], 1, 1) + dot(d_u, wu[...], 1, 1)
+        dgu[g, j, :, :hidden] = d_g
+        dgu[g, j, :, hidden:] = d_u
+        value = dot(d_g, wg_t[...], 1, 0) + dot(d_u, wu_t[...], 1, 0)
         dx_part[g, j] = value.astype(BF16).reshape(2, CAP, wide)
         dx_copy(g, j).start()
 
-    def join_unit(g, j):
+    def join_unit(g, j, leave=True):
         dx_copy(g, j).wait_recv()
-        dx_sum[g, j] = (dx_part[g, j, c].astype(F32) + dx_recv[g, j].astype(F32)).astype(BF16)
+        total = (dx_part[g, j, c].astype(F32) + dx_recv[g, j].astype(F32)).astype(BF16)
 
         if j == 1:
-            home[g, j] = dx_sum[g, j]
+            home[g, j] = total
         else:
-            home_copy(g, j // 2).start()
-
-    def unpack(g, target):
+            dx_part[g, j, c] = total
+            if leave:
+                home_copy(g, j // 2).start()
+
+    def arrive(g):
         for k in range(2):
             home_copy(g, k).wait_recv()
+
+    def unpack(g, target):
         tokens = sel.shape[3]
         target[...] = dot(
             sel[g].reshape(3 * CAP, tokens), home[g].reshape(3 * CAP, wide), 0, 0
@@ -290,6 +296,8 @@
 
     first(0, 1)
     x_pre(0, 1).start()
+    for plain, turned in ((wg, wg_t), (wu, wu_t)):
+        turned[...] = plain[...].T
     x_facts.wait_recv()
     x_tok.wait_recv()
     front(1, far_tok)
@@ -333,18 +341,20 @@
     down_unit(0, 0)
     down_unit(1, 1)
     join_unit(1, 1)
+    join_unit(0, 0, leave=False)
+    arrive(1)
+    home_copy(0, 0).start()
     unpack(1, res_far)
     x_res.start()
-    join_unit(0, 0)
     down_unit(0, 2)
+    join_unit(0, 2)
     down_unit(0, 1)
-    join_unit(0, 2)
     join_unit(0, 1)
-    grad_unit(2, back, hid, out_down)
-    grad_unit(0, rows, dgate, out_gate)
-    grad_unit(1, rows, dup, out_up)
-    unpack(0, res_near)
-    near_out = pltpu.make_async_copy(res_near, out_tok.at[:, mine], near_sem)
+    grad_unit(back, hid, ((2, out_down),))
+    grad_unit(rows, dgu, ((0, out_gate), (1, out_up)))
+    arrive(0)
+    unpack(0, near_tok)
+    near_out = pltpu.make_async_copy(near_tok, out_tok.at[:, mine], near_sem)
     near_out.start()
 
     x_tok.wait_send()
@@ -391,7 +401,7 @@
         copy.wait()
 
 
-def settled(arrays, parts=4):
+def settled(arrays, parts=2):
     return pl.pallas_call(
         functools.partial(settle_kernel, parts),
         out_shape=tuple(jax.ShapeDtypeStruct(a.shape, a.dtype) for a in arrays),
@@ -435,6 +445,8 @@
             vmem((wide, hidden), BF16),
             vmem((wide, hidden), BF16),
             vmem((wide, hidden), BF16),
+            vmem((hidden, wide), BF16),
+            vmem((hidden, wide), BF16),
             vmem((count, wide), BF16),
             vmem((count, wide), BF16),
             vmem((2, 3, 2, 8, count), F32),
@@ -452,13 +464,10 @@
             vmem((2, 3, units, hidden), F32),
             vmem((2, 3, units, hidden), BF16),
             vmem((2, 3, units, hidden), BF16),
-            vmem((2, 3, units, hidden), BF16),
-            vmem((2, 3, units, hidden), BF16),
+            vmem((2, 3, units, 2 * hidden), BF16),
             vmem((2, 3, 2, CAP, wide), BF16),
             vmem((2, 3, CAP, wide), BF16),
             vmem((2, 3, CAP, wide), BF16),
-            vmem((2, 3, CAP, wide), BF16),
-            vmem((count, wide), BF16),
             vmem((count, wide), BF16),
             vmem((3, wide, hidden), BF16),
             dma((6,)),

time: 84 us -> 82.8 us (0.986)
  Pallas kernels: 83.1 us -> 81.8 us
    pallas_call x1, Pallas kernels: 80.2 us -> 79 us  [per_device(): pl.pallas_call(functools.partial(kernel, n_blk), out_shape=(jax.ShapeDtyp...]
where the time goes in v3:
time: 82.8 us; the launch traced here: 82.6 us
  Pallas kernels  81.8 us (99%)
    pallas_call x1, Pallas kernels, per_device(): pl.pallas_call(functools.partial(kernel, n_blk), out_shape=(jax.ShapeDtyp...  79 us
    pallas_call x1, Pallas kernels, settled(): pl.pallas_call(functools.partial(settle_kernel, parts), out_shape=tuple((...  2.78 us

profile of v3, /device:TPU:0, one launch (start us, length us, event | category | flops | bytes accessed | tf_op | source)
XLA Modules:
  0.0 82.6 jit_solution(4909142698961937009)
XLA Ops:
  0.6 79.0 %shard_map.93 = (bf16[128,3584]{1,0:T(8,128)(2,1)S(1)}, bf16[1792,512]{1,0:T(8,128)(2,1)S(1)}, bf16[1792,512]{1,0:T(8,128)(2,1)S(1)}, bf16[1792,512]{1,0:T(8,128)(2,1)S(1)}) custom-call(bf16[128,3584]{1,0:T(8,128)(2,1)} %tok.1, s32[1,128]{1,0:T(1,128)} %bitcast.11, f32[1,128]{1,0:T(1,128)} %bitcast.12, bf16[1792,512]{1,0:T(8,128)(2,1)} %bitcast.8, ...), custom_call_target="tpu_custom_call" | custom-call | tf_op jit(solution)/shard_map/pallas_call | solution.py:425
  79.7 2.8 %shard_map.94 = (bf16[128,3584]{1,0:T(8,128)(2,1)}, bf16[1792,512]{1,0:T(8,128)(2,1)}, bf16[1792,512]{1,0:T(8,128)(2,1)}, bf16[1792,512]{1,0:T(8,128)(2,1)}) custom-call(bf16[128,3584]{1,0:T(8,128)(2,1)S(1)} %get-tuple-element.12.refs_0_, bf16[1792,512]{1,0:T(8,128)(2,1)S(1)} %get-tuple-element.13.refs_1_, bf16[1792,512]{1,0:T(8,128)(2,1)S(1)} %get-tuple-element.14.refs_2_, ...), custom_call_target="tpu_custom_call" | custom-call | tf_op jit(solution)/shard_map/pallas_call | solution.py:405

commit v4 on v3

--- a/solution.py
+++ b/solution.py
@@ -328,26 +328,26 @@
     activate(0, 2)
     back_unit(0, 2)
     x_dh(0, 2).start()
-    x_dh(1, 0).start()
+    x_dh(1, 2).start()
     down_unit(1, 0)
     join_unit(1, 0)
     activate(0, 1)
     back_unit(0, 1)
     x_dh(0, 1).start()
-    x_dh(1, 2).start()
+    x_dh(1, 0).start()
     x_dh(1, 1).start()
     down_unit(1, 2)
     join_unit(1, 2)
-    down_unit(0, 0)
+    down_unit(0, 2)
     down_unit(1, 1)
     join_unit(1, 1)
-    join_unit(0, 0, leave=False)
+    join_unit(0, 2, leave=False)
     arrive(1)
-    home_copy(0, 0).start()
+    home_copy(0, 1).start()
     unpack(1, res_far)
     x_res.start()
-    down_unit(0, 2)
-    join_unit(0, 2)
+    down_unit(0, 0)
+    join_unit(0, 0)
     down_unit(0, 1)
     join_unit(0, 1)
     grad_unit(back, hid, ((2, out_down),))

time: 82.8 us -> 81.3 us (0.982)
  Pallas kernels: 81.8 us -> 80.4 us
    pallas_call x1, Pallas kernels: 79 us -> 77.6 us  [per_device(): pl.pallas_call(functools.partial(kernel, n_blk), out_shape=(jax.ShapeDtyp...]
where the time goes in v4:
time: 81.3 us; the launch traced here: 81.2 us
  Pallas kernels  80.4 us (99%)
    pallas_call x1, Pallas kernels, per_device(): pl.pallas_call(functools.partial(kernel, n_blk), out_shape=(jax.ShapeDtyp...  77.6 us
    pallas_call x1, Pallas kernels, settled(): pl.pallas_call(functools.partial(settle_kernel, parts), out_shape=tuple((...  2.78 us

profile of v4, /device:TPU:0, one launch (start us, length us, event | category | flops | bytes accessed | tf_op | source)
XLA Modules:
  0.0 81.2 jit_solution(5999906502634775302)
XLA Ops:
  0.6 77.6 %shard_map.93 = (bf16[128,3584]{1,0:T(8,128)(2,1)S(1)}, bf16[1792,512]{1,0:T(8,128)(2,1)S(1)}, bf16[1792,512]{1,0:T(8,128)(2,1)S(1)}, bf16[1792,512]{1,0:T(8,128)(2,1)S(1)}) custom-call(bf16[128,3584]{1,0:T(8,128)(2,1)} %tok.1, s32[1,128]{1,0:T(1,128)} %bitcast.11, f32[1,128]{1,0:T(1,128)} %bitcast.12, bf16[1792,512]{1,0:T(8,128)(2,1)} %bitcast.8, ...), custom_call_target="tpu_custom_call" | custom-call | tf_op jit(solution)/shard_map/pallas_call | solution.py:425
  78.2 2.8 %shard_map.94 = (bf16[128,3584]{1,0:T(8,128)(2,1)}, bf16[1792,512]{1,0:T(8,128)(2,1)}, bf16[1792,512]{1,0:T(8,128)(2,1)}, bf16[1792,512]{1,0:T(8,128)(2,1)}) custom-call(bf16[128,3584]{1,0:T(8,128)(2,1)S(1)} %get-tuple-element.12.refs_0_, bf16[1792,512]{1,0:T(8,128)(2,1)S(1)} %get-tuple-element.13.refs_1_, bf16[1792,512]{1,0:T(8,128)(2,1)S(1)} %get-tuple-element.14.refs_2_, ...), custom_call_target="tpu_custom_call" | custom-call | tf_op jit(solution)/shard_map/pallas_call | solution.py:405
